TPU v7x, 32 devices: a whole 2x2x4 slice. The times are simulated.
32 devices in a mesh: layer: 4 (over y, x), col: 8 (over z, core).
Axes of the slice: x: 2, y: 2, z: 4, core: 2. Of those that a mesh axis runs over, the one named last changes fastest.
Arguments:
- inputs: bfloat16 [4, 128, 4096], replicated, may hold values from -6 to 6
- w_input: bfloat16 [4, 4096, 4, 4096], P('layer', None, None, 'col'), may hold values from -0.09375 to 0.09375
- w_recur: bfloat16 [4, 4096, 4, 4096], P('layer', None, None, 'col'), may hold values from -0.09375 to 0.09375
- bias: float32 [4, 4, 4096], P('layer', None, 'col'), may hold values from -1 to 2
- h_start: bfloat16 [4, 128, 4096], P('layer', None, 'col'), may hold values from -3 to 3
- c_start: float32 [4, 128, 4096], P('layer', None, 'col'), may hold values from -6 to 6
Outputs:
- hidden_seq: bfloat16 [4, 4, 128, 4096], P('layer', None, None, 'col')
- cell_final: float32 [4, 128, 4096], P('layer', None, 'col')
All inputs are finite; a program needn't handle non-finite values.
Results may differ from a plain program's by a relative error of at most 0.0024.
Values may be sent and summed in bfloat16 or wider, within the bound.
A program may use at most 128 MiB of HBM per device.

v0:
```python
import jax
import jax.numpy as jnp
from jax import lax
from jax.sharding import PartitionSpec as P


def passed_along(value, axis, steps):
    count = lax.axis_size(axis)
    first, last = (max(0, -steps), min(count, count - steps))
    return lax.ppermute(value, axis, [(source, source + steps) for source in range(first, last)])


def body(inputs, w_input, w_recur, bias, h_start, c_start):
    steps = inputs.shape[0]
    batch = inputs.shape[1]
    width = inputs.shape[2]
    local = w_input.shape[3]
    span = steps // 4
    count = steps // span
    groups = lax.axis_size("layer")
    rounds = count + groups - 1
    section = lax.axis_index("layer")
    weight_in = w_input[0].reshape(width, 4 * local)
    weight_rec = w_recur[0].reshape(width, 4 * local)
    offset = bias[0].reshape(4 * local)
    hidden_full = lax.all_gather(h_start[0], "col", axis=1, tiled=True)
    cell = c_start[0]
    sequence = jnp.zeros((steps, batch, local), jnp.bfloat16)
    arrived = jnp.zeros((span, batch, width), jnp.bfloat16)

    def advance(carry, z_in):
        hidden_prev, cell_prev = carry
        gates = z_in + jnp.dot(hidden_prev, weight_rec, preferred_element_type=jnp.float32)
        gates = gates.reshape(batch, 4, local)
        cell_new = jax.nn.sigmoid(gates[:, 1]) * cell_prev + jax.nn.sigmoid(gates[:, 0]) * jnp.tanh(
            gates[:, 2]
        )
        hidden_new = (jax.nn.sigmoid(gates[:, 3]) * jnp.tanh(cell_new)).astype(jnp.bfloat16)
        hidden_wide = lax.all_gather(hidden_new, "col", axis=1, tiled=True)
        return ((hidden_wide, cell_new), (hidden_new, hidden_wide))

    for turn in range(rounds):
        block_id = turn - section
        valid = jnp.logical_and(block_id >= 0, block_id < count)
        start = jnp.clip(block_id, 0, count - 1) * span
        own_block = lax.dynamic_slice_in_dim(inputs, start, span, 0)
        source = jnp.where(section == 0, own_block, arrived)
        projected = (
            jnp.dot(
                source.reshape(span * batch, width), weight_in, preferred_element_type=jnp.float32
            )
            + offset
        )
        projected = projected.reshape(span, batch, 4 * local)
        (hidden_next, cell_next), (shards, wides) = lax.scan(
            advance, (hidden_full, cell), projected
        )
        hidden_full = jnp.where(valid, hidden_next, hidden_full)
        cell = jnp.where(valid, cell_next, cell)
        sequence = jnp.where(
            valid, lax.dynamic_update_slice_in_dim(sequence, shards, start, 0), sequence
        )
        if turn + 1 < rounds:
            received = passed_along(shards, "layer", 1)
            arrived = lax.all_gather(received, "col", axis=2, tiled=True)
    return (sequence[None], cell[None])


def solution(mesh):
    in_specs = (
        P(),
        P("layer", None, None, "col"),
        P("layer", None, None, "col"),
        P("layer", None, "col"),
        P("layer", None, "col"),
        P("layer", None, "col"),
    )
    out_specs = (P("layer", None, None, "col"), P("layer", None, "col"))
    return jax.shard_map(body, mesh=mesh, in_specs=in_specs, out_specs=out_specs, check_vma=False)
```

profile of v0, /device:TPU:0, one launch (start us, length us, event | category | flops | bytes accessed | tf_op | source)
XLA Modules:
  0.0 451.5 jit_solution(1819920880127915274)
XLA Ops:
  8.7 18.2 %copy.64 = bf16[512,8,4,512]{3,1,2,0:T(8,128)(2,1)} copy(bf16[512,8,4,512]{3,2,1,0:T(4,128)(2,1)} %bitcast.365) | data formatting | bytes 33554432
  26.8 9.5 %copy.66 = bf16[512,8,4,512]{3,1,2,0:T(8,128)(2,1)} copy(bf16[512,8,4,512]{3,2,1,0:T(4,128)(2,1)S(1)} %bitcast.366) | data formatting | bytes 33554432
  36.4 8.4 %convolution_add_fusion.7 = f32[128,2048]{1,0:T(8,128)S(1)} fusion(bf16[4096,2048]{1,0:T(8,128)(2,1)} %bitcast.351, bf16[4,128,4096]{2,1,0:T(8,128)(2,1)} %param.6, s32[]{:T(128)S(6)} %min.22, pred[]{:T(512)S(6)} %eq.2, f32[2048]{0:T(1024)S(1)} %bitcast.368), kind=kOutput, calls=%fused_computation.13 | convolution fusion | flops 2148270080 | bytes 18882564 | tf_op jit(solution)/shard_map/dot_general | solution.py:49
  44.9 8.5 %convolution_add_fusion.6 = f32[128,2048]{1,0:T(8,128)S(1)} fusion(f32[128,2048]{1,0:T(8,128)S(1)} %convolution_add_fusion.7, bf16[4096,2048]{1,0:T(8,128)(2,1)} %bitcast.358, bf16[1,128,4096]{2,1,0:T(8,128)(2,1)} %all-gather.39.cloned.1.call-done), kind=kOutput, calls=%fused_computation.12 | convolution fusion | flops 2147745792 | bytes 19922944 | tf_op jit(solution)/shard_map/while/body/eval_jaxpr/dot_general | solution.py:33
  56.1 4.8 %collective-permute-start = (bf16[1,128,512]{2,1,0:T(8,128)(2,1)S(1)}, bf16[1,128,512]{2,1,0:T(8,128)(2,1)S(1)}, u32[]{:S(2)}, u32[]{:S(2)}) collective-permute-start(bf16[1,128,512]{2,1,0:T(8,128)(2,1)S(1)} %get-tuple-element.137), channel_id=1, source_target_pairs={{0,8},{8,16},{16,24},{1,9},{9,17},{17,25},{2,10},{10,18},{18,26},{... | collective-permute-start | bytes 393224 | tf_op jit(solution)/shard_map/ppermute | solution.py:10
  64.6 16.3 %all-gather.17.cloned.1.call-done = bf16[128,4096]{1,0:T(8,128)(2,1)} async-done(((bf16[128,512]{1,0:T(8,128)(2,1)}), bf16[128,4096]{1,0:T(8,128)(2,1)}) %all-gather.17.cloned.1.call-update) | async-done | bytes 1048592 | tf_op jit(solution)/shard_map/while/body/eval_jaxpr/all_gather | solution.py:39
  82.5 9.1 %fusion.159 = f32[128,2048]{1,0:T(8,128)} fusion(bf16[128,4096]{1,0:T(8,128)(2,1)S(1)} %bitcast_select_fusion, bf16[4096,2048]{1,0:T(8,128)(2,1)} %bitcast.359), kind=kOutput, calls=%fused_computation.241 | convolution fusion | flops 2147483648 | bytes 18874368 | tf_op jit(solution)/shard_map/while/body/eval_jaxpr/dot_general | solution.py:33
  91.6 13.3 %all-gather.15.cloned.1.call-done = bf16[1,128,4096]{2,1,0:T(8,128)(2,1)} async-done(((bf16[1,128,512]{2,1,0:T(8,128)(2,1)}), bf16[1,128,4096]{2,1,0:T(8,128)(2,1)}) %all-gather.15.cloned.1.call-update) | async-done | bytes 1048592 | tf_op jit(solution)/shard_map/all_gather | solution.py:65
  104.9 9.7 %fusion.5 = f32[128,2048]{1,0:T(8,128)} fusion(f32[128,2048]{1,0:T(8,128)} %fusion.159, bf16[4096,2048]{1,0:T(8,128)(2,1)} %bitcast.352, bf16[1,128,4096]{2,1,0:T(8,128)(2,1)} %all-gather.15.cloned.1.call-done, bf16[4,128,4096]{2,1,0:T(8,128)(2,1)} %param.6, s32[]{:T(128)S(6)} %min.23, pred[]{:T(512)S(6)} %eq.2, f32[2048]{0:T(1024)S(1)} %bitcast.369), kind=kOutput, calls=%fused_computation.11 | convolution fusion | flops 2148532224 | bytes 20979716 | tf_op jit(solution)/shard_map/dot_general | solution.py:49
  117.5 3.5 fusion.157
  122.4 3.7 collective-permute-start.1
  126.1 3.1 collective-permute-done.1
  130.2 14.4 %all-gather.21.cloned.1.call-done = bf16[128,4096]{1,0:T(8,128)(2,1)} async-done(((bf16[128,512]{1,0:T(8,128)(2,1)}), bf16[128,4096]{1,0:T(8,128)(2,1)}) %all-gather.21.cloned.1.call-update) | async-done | bytes 1048592 | tf_op jit(solution)/shard_map/while/body/eval_jaxpr/all_gather | solution.py:39
  144.6 9.5 %fusion.39 = f32[128,2048]{1,0:T(8,128)} fusion(bf16[4096,2048]{1,0:T(8,128)(2,1)} %bitcast.360, bf16[128,4096]{1,0:T(8,128)(2,1)} %all-gather.21.cloned.1.call-done, bf16[128,4096]{1,0:T(8,128)(2,1)S(1)} %bitcast_select_fusion, pred[]{:T(512)S(6)} %and.23), kind=kOutput, calls=%fused_computation.52 | convolution fusion | flops 2148007936 | bytes 19922944 | tf_op jit(solution)/shard_map/while/body/eval_jaxpr/dot_general | solution.py:33
  154.0 13.9 %all-gather.19.cloned.1.call-done = bf16[1,128,4096]{2,1,0:T(8,128)(2,1)} async-done(((bf16[1,128,512]{2,1,0:T(8,128)(2,1)}), bf16[1,128,4096]{2,1,0:T(8,128)(2,1)}) %all-gather.19.cloned.1.call-update) | async-done | bytes 1048592 | tf_op jit(solution)/shard_map/all_gather | solution.py:65
  167.9 9.7 %fusion.4 = f32[128,2048]{1,0:T(8,128)} fusion(f32[128,2048]{1,0:T(8,128)} %fusion.39, bf16[4096,2048]{1,0:T(8,128)(2,1)} %bitcast.353, bf16[1,128,4096]{2,1,0:T(8,128)(2,1)} %all-gather.19.cloned.1.call-done, bf16[4,128,4096]{2,1,0:T(8,128)(2,1)} %param.6, s32[]{:T(128)S(6)} %min.24, pred[]{:T(512)S(6)} %eq.2, f32[2048]{0:T(1024)S(1)} %bitcast.370), kind=kOutput, calls=%fused_computation.9 | convolution fusion | flops 2148532224 | bytes 20979716 | tf_op jit(solution)/shard_map/dot_general | solution.py:49
  177.6 2.9 reshape.903
  180.5 3.9 fusion.156
  189.2 3.7 collective-permute-start.2
  192.9 3.1 collective-permute-done.2
  197.0 12.5 %all-gather.25.cloned.1.call-done = bf16[128,4096]{1,0:T(8,128)(2,1)} async-done(((bf16[128,512]{1,0:T(8,128)(2,1)}), bf16[128,4096]{1,0:T(8,128)(2,1)}) %all-gather.25.cloned.1.call-update) | async-done | bytes 1048592 | tf_op jit(solution)/shard_map/while/body/eval_jaxpr/all_gather | solution.py:39
  211.1 9.1 %fusion.160 = f32[128,2048]{1,0:T(8,128)} fusion(bf16[128,4096]{1,0:T(8,128)(2,1)S(1)} %broadcast_select_fusion.2, bf16[4096,2048]{1,0:T(8,128)(2,1)} %bitcast.361), kind=kOutput, calls=%fused_computation.242 | convolution fusion | flops 2147483648 | bytes 18874368 | tf_op jit(solution)/shard_map/while/body/eval_jaxpr/dot_general | solution.py:33
  220.2 12.7 %all-gather.23.cloned.1.call-done = bf16[1,128,4096]{2,1,0:T(8,128)(2,1)} async-done(((bf16[1,128,512]{2,1,0:T(8,128)(2,1)}), bf16[1,128,4096]{2,1,0:T(8,128)(2,1)}) %all-gather.23.cloned.1.call-update) | async-done | bytes 1048592 | tf_op jit(solution)/shard_map/all_gather | solution.py:65
  232.9 9.7 %fusion.3 = f32[128,2048]{1,0:T(8,128)} fusion(f32[128,2048]{1,0:T(8,128)} %fusion.160, bf16[4096,2048]{1,0:T(8,128)(2,1)} %bitcast.354, bf16[1,128,4096]{2,1,0:T(8,128)(2,1)} %all-gather.23.cloned.1.call-done, bf16[4,128,4096]{2,1,0:T(8,128)(2,1)} %param.6, s32[]{:T(128)S(6)} %min.25, pred[]{:T(512)S(6)} %eq.2, f32[2048]{0:T(1024)S(1)} %bitcast.371), kind=kOutput, calls=%fused_computation.7 | convolution fusion | flops 2148532224 | bytes 20979716 | tf_op jit(solution)/shard_map/dot_general | solution.py:49
  242.6 2.9 reshape.905
  245.5 3.9 fusion.155
  253.0 3.7 collective-permute-start.3
  256.7 3.1 collective-permute-done.3
  261.0 13.0 %all-gather.29.cloned.1.call-done = bf16[128,4096]{1,0:T(8,128)(2,1)} async-done(((bf16[128,512]{1,0:T(8,128)(2,1)}), bf16[128,4096]{1,0:T(8,128)(2,1)}) %all-gather.29.cloned.1.call-update) | async-done | bytes 1048592 | tf_op jit(solution)/shard_map/while/body/eval_jaxpr/all_gather | solution.py:39
  274.0 9.5 %fusion.40 = f32[128,2048]{1,0:T(8,128)} fusion(bf16[4096,2048]{1,0:T(8,128)(2,1)} %bitcast.362, bf16[128,4096]{1,0:T(8,128)(2,1)} %all-gather.29.cloned.1.call-done, bf16[128,4096]{1,0:T(8,128)(2,1)S(1)} %broadcast_select_fusion.2, pred[]{:T(512)S(6)} %and.25), kind=kOutput, calls=%fused_computation.53 | convolution fusion | flops 2148007936 | bytes 19922944 | tf_op jit(solution)/shard_map/while/body/eval_jaxpr/dot_general | solution.py:33
  283.5 14.6 %all-gather.27.cloned.1.call-done = bf16[1,128,4096]{2,1,0:T(8,128)(2,1)} async-done(((bf16[1,128,512]{2,1,0:T(8,128)(2,1)}), bf16[1,128,4096]{2,1,0:T(8,128)(2,1)}) %all-gather.27.cloned.1.call-update) | async-done | bytes 1048592 | tf_op jit(solution)/shard_map/all_gather | solution.py:65
  298.1 9.7 %fusion.2 = f32[128,2048]{1,0:T(8,128)} fusion(f32[128,2048]{1,0:T(8,128)} %fusion.40, bf16[4096,2048]{1,0:T(8,128)(2,1)} %bitcast.355, bf16[1,128,4096]{2,1,0:T(8,128)(2,1)} %all-gather.27.cloned.1.call-done, bf16[4,128,4096]{2,1,0:T(8,128)(2,1)} %param.6, s32[]{:T(128)S(6)} %min.26, pred[]{:T(512)S(6)} %eq.2, f32[2048]{0:T(1024)S(1)} %bitcast.372), kind=kOutput, calls=%fused_computation.5 | convolution fusion | flops 2148532224 | bytes 20979716 | tf_op jit(solution)/shard_map/dot_general | solution.py:49
  307.8 2.9 reshape.907
  310.7 3.9 fusion.154
  319.4 3.7 collective-permute-start.4
  323.1 3.1 collective-permute-done.4
  327.1 12.5 %all-gather.33.cloned.1.call-done = bf16[128,4096]{1,0:T(8,128)(2,1)} async-done(((bf16[128,512]{1,0:T(8,128)(2,1)}), bf16[128,4096]{1,0:T(8,128)(2,1)}) %all-gather.33.cloned.1.call-update) | async-done | bytes 1048592 | tf_op jit(solution)/shard_map/while/body/eval_jaxpr/all_gather | solution.py:39
  341.0 9.1 %fusion.161 = f32[128,2048]{1,0:T(8,128)} fusion(bf16[128,4096]{1,0:T(8,128)(2,1)S(1)} %broadcast_select_fusion, bf16[4096,2048]{1,0:T(8,128)(2,1)} %bitcast.363), kind=kOutput, calls=%fused_computation.243 | convolution fusion | flops 2147483648 | bytes 18874368 | tf_op jit(solution)/shard_map/while/body/eval_jaxpr/dot_general | solution.py:33
  350.1 13.0 %all-gather.31.cloned.1.call-done = bf16[1,128,4096]{2,1,0:T(8,128)(2,1)} async-done(((bf16[1,128,512]{2,1,0:T(8,128)(2,1)}), bf16[1,128,4096]{2,1,0:T(8,128)(2,1)}) %all-gather.31.cloned.1.call-update) | async-done | bytes 1048592 | tf_op jit(solution)/shard_map/all_gather | solution.py:65
  363.1 9.7 %fusion.1 = f32[128,2048]{1,0:T(8,128)} fusion(f32[128,2048]{1,0:T(8,128)} %fusion.161, bf16[4096,2048]{1,0:T(8,128)(2,1)} %bitcast.356, bf16[1,128,4096]{2,1,0:T(8,128)(2,1)} %all-gather.31.cloned.1.call-done, bf16[4,128,4096]{2,1,0:T(8,128)(2,1)} %param.6, s32[]{:T(128)S(6)} %min.27, pred[]{:T(512)S(6)} %eq.2, f32[2048]{0:T(1024)S(1)} %bitcast.373), kind=kOutput, calls=%fused_computation.3 | convolution fusion | flops 2148532224 | bytes 20979716 | tf_op jit(solution)/shard_map/dot_general | solution.py:49
  372.8 2.9 reshape.909
  375.7 3.9 fusion.153
  383.9 3.9 collective-permute-start.5
  392.2 12.6 %all-gather.37.cloned.1.call-done = bf16[128,4096]{1,0:T(8,128)(2,1)} async-done(((bf16[128,512]{1,0:T(8,128)(2,1)}), bf16[128,4096]{1,0:T(8,128)(2,1)}) %all-gather.37.cloned.1.call-update) | async-done | bytes 1048592 | tf_op jit(solution)/shard_map/while/body/eval_jaxpr/all_gather | solution.py:39
  404.7 9.1 %fusion.14 = f32[128,2048]{1,0:T(8,128)} fusion(bf16[4096,2048]{1,0:T(8,128)(2,1)} %bitcast.364, bf16[128,4096]{1,0:T(8,128)(2,1)} %all-gather.37.cloned.1.call-done, bf16[128,4096]{1,0:T(8,128)(2,1)S(1)} %broadcast_select_fusion, pred[]{:T(512)S(6)} %and.27), kind=kOutput, calls=%fused_computation.23 | convolution fusion | flops 2148007936 | bytes 19922944 | tf_op jit(solution)/shard_map/while/body/eval_jaxpr/dot_general | solution.py:33
  413.9 14.9 %all-gather.35.cloned.1.call-done = bf16[1,128,4096]{2,1,0:T(8,128)(2,1)} async-done(((bf16[1,128,512]{2,1,0:T(8,128)(2,1)}), bf16[1,128,4096]{2,1,0:T(8,128)(2,1)}) %all-gather.35.cloned.1.call-update) | async-done | bytes 1048592 | tf_op jit(solution)/shard_map/all_gather | solution.py:65
  428.8 8.8 %fusion = f32[128,2048]{1,0:T(8,128)S(1)} fusion(f32[128,2048]{1,0:T(8,128)} %fusion.14, bf16[4096,2048]{1,0:T(8,128)(2,1)} %bitcast.357, bf16[1,128,4096]{2,1,0:T(8,128)(2,1)} %all-gather.35.cloned.1.call-done, bf16[4,128,4096]{2,1,0:T(8,128)(2,1)} %param.6, s32[]{:T(128)S(6)} %min.28, pred[]{:T(512)S(6)} %eq.2, f32[2048]{0:T(1024)S(1)} %bitcast.374), kind=kOutput, calls=%fused_computation.1 | convolution fusion | flops 2148532224 | bytes 20979716 | tf_op jit(solution)/shard_map/dot_general | solution.py:49
  439.2 3.6 fusion.152
  (107 shorter events, 45.8 us)
Async XLA Ops:
  7.2 37.7 %all-gather.39.cloned.1.call-start = ((), (), s32[]{:S(2)}) async-start(), calls=%async_computation.12 | async-start | bytes 1179648 | tf_op jit(solution)/shard_map/all_gather | solution.py:26
  7.9 73.0 %all-gather.17.cloned.1.call-start = ((), (), s32[]{:S(2)}) async-start(), calls=%async_computation.1 | async-start | bytes 1179648 | tf_op jit(solution)/shard_map/while/body/eval_jaxpr/all_gather | solution.py:39
  8.7 18.2 %copy-start = (bf16[1,4096,4,512]{3,2,1,0:T(4,128)(2,1)S(1)}, bf16[1,4096,4,512]{3,2,1,0:T(4,128)(2,1)}, u32[]{:S(2)}) copy-start(bf16[1,4096,4,512]{3,2,1,0:T(4,128)(2,1)} %param.8) | copy-start | bytes 50331652
  44.8 10.0 %copy-start.3 = (f32[1,128,512]{2,1,0:T(8,128)S(1)}, f32[1,128,512]{2,1,0:T(8,128)}, u32[]{:S(2)}) copy-start(f32[1,128,512]{2,1,0:T(8,128)} %param.11) | copy-start | bytes 786436
  55.8 49.1 %all-gather.15.cloned.1.call-start = ((), (), s32[]{:S(2)}) async-start(), calls=%async_computation | async-start | bytes 1179648 | tf_op jit(solution)/shard_map/all_gather | solution.py:65
  56.1 7.6 %collective-permute-start = (bf16[1,128,512]{2,1,0:T(8,128)(2,1)S(1)}, bf16[1,128,512]{2,1,0:T(8,128)(2,1)S(1)}, u32[]{:S(2)}, u32[]{:S(2)}) collective-permute-start(bf16[1,128,512]{2,1,0:T(8,128)(2,1)S(1)} %get-tuple-element.137), channel_id=1, source_target_pairs={{0,8},{8,16},{16,24},{1,9},{9,17},{17,25},{2,10},{10,18},{18,26},{... | collective-permute-start | bytes 393224 | tf_op jit(solution)/shard_map/ppermute | solution.py:10
  63.7 0.7 copy-start.23
  64.4 80.2 %all-gather.21.cloned.1.call-start = ((), (), s32[]{:S(2)}) async-start(), calls=%async_computation.3 | async-start | bytes 1179648 | tf_op jit(solution)/shard_map/while/body/eval_jaxpr/all_gather | solution.py:39
  122.0 65.2 %copy-start.4 = (f32[128,1,512]{2,0,1:T(8,128)}, f32[128,1,512]{2,0,1:T(8,128)S(1)}, u32[]{:S(2)}) copy-start(f32[128,1,512]{2,0,1:T(8,128)S(1)} %get-tuple-element.125) | copy-start | bytes 786436
  122.1 45.8 %all-gather.19.cloned.1.call-start = ((), (), s32[]{:S(2)}) async-start(), calls=%async_computation.2 | async-start | bytes 1179648 | tf_op jit(solution)/shard_map/all_gather | solution.py:65
  122.4 6.8 %collective-permute-start.1 = (bf16[1,128,512]{2,1,0:T(8,128)(2,1)S(1)}, bf16[1,128,512]{2,1,0:T(8,128)(2,1)S(1)}, u32[]{:S(2)}, u32[]{:S(2)}) collective-permute-start(bf16[1,128,512]{2,1,0:T(8,128)(2,1)S(1)} %get-tuple-element.133), channel_id=1, source_target_pairs={{0,8},{8,16},{16,24},{1,9},{9,17},{17,25},{2,10},{10,18},{18,26},{... | collective-permute-start | bytes 393224 | tf_op jit(solution)/shard_map/ppermute | solution.py:10
  129.2 0.6 copy-start.25
  129.9 79.6 %all-gather.25.cloned.1.call-start = ((), (), s32[]{:S(2)}) async-start(), calls=%async_computation.5 | async-start | bytes 1179648 | tf_op jit(solution)/shard_map/while/body/eval_jaxpr/all_gather | solution.py:39
  184.5 0.7 copy-start.18
  187.1 45.8 %all-gather.23.cloned.1.call-start = ((), (), s32[]{:S(2)}) async-start(), calls=%async_computation.4 | async-start | bytes 1179648 | tf_op jit(solution)/shard_map/all_gather | solution.py:65
  189.2 7.8 %copy-start.6 = (bf16[4,128,512]{2,1,0:T(8,128)(2,1)}, bf16[4,128,512]{2,1,0:T(8,128)(2,1)S(1)}, u32[]{:S(2)}) copy-start(bf16[4,128,512]{2,1,0:T(8,128)(2,1)S(1)} %get-tuple-element.120) | copy-start | bytes 1572868
  189.2 6.8 %collective-permute-start.2 = (bf16[1,128,512]{2,1,0:T(8,128)(2,1)S(1)}, bf16[1,128,512]{2,1,0:T(8,128)(2,1)S(1)}, u32[]{:S(2)}, u32[]{:S(2)}) collective-permute-start(bf16[1,128,512]{2,1,0:T(8,128)(2,1)S(1)} %get-tuple-element.121), channel_id=1, source_target_pairs={{0,8},{8,16},{16,24},{1,9},{9,17},{17,25},{2,10},{10,18},{18,26},{... | collective-permute-start | bytes 393224 | tf_op jit(solution)/shard_map/ppermute | solution.py:10
  196.0 0.6 copy-start.24
  196.7 77.3 %all-gather.29.cloned.1.call-start = ((), (), s32[]{:S(2)}) async-start(), calls=%async_computation.7 | async-start | bytes 1179648 | tf_op jit(solution)/shard_map/while/body/eval_jaxpr/all_gather | solution.py:39
  220.2 29.2 %copy-start.5 = (f32[128,1,512]{2,0,1:T(8,128)S(1)}, f32[128,1,512]{2,0,1:T(8,128)}, u32[]{:S(2)}) copy-start(f32[128,1,512]{2,0,1:T(8,128)} %copy-done.4) | copy-start | bytes 786436
  220.2 31.5 %copy-start.7 = (bf16[4,128,512]{2,1,0:T(8,128)(2,1)S(1)}, bf16[4,128,512]{2,1,0:T(8,128)(2,1)}, u32[]{:S(2)}) copy-start(bf16[4,128,512]{2,1,0:T(8,128)(2,1)} %copy-done.6) | copy-start | bytes 1572868
  220.2 31.5 %copy-start.14 = (f32[1,128,512]{2,1,0:T(8,128)S(1)}, f32[1,128,512]{2,1,0:T(8,128)}, u32[]{:S(2)}) copy-start(f32[1,128,512]{2,1,0:T(8,128)} %get-tuple-element.122) | copy-start | bytes 786436
  249.5 2.2 copy-start.20
  251.7 65.7 %copy-start.1 = (f32[128,1,512]{2,0,1:T(8,128)}, f32[128,1,512]{2,0,1:T(8,128)S(1)}, u32[]{:S(2)}) copy-start(f32[128,1,512]{2,0,1:T(8,128)S(1)} %get-tuple-element.109) | copy-start | bytes 786436
  251.7 46.4 %all-gather.27.cloned.1.call-start = ((), (), s32[]{:S(2)}) async-start(), calls=%async_computation.6 | async-start | bytes 1179648 | tf_op jit(solution)/shard_map/all_gather | solution.py:65
  253.0 6.8 %collective-permute-start.3 = (bf16[1,128,512]{2,1,0:T(8,128)(2,1)S(1)}, bf16[1,128,512]{2,1,0:T(8,128)(2,1)S(1)}, u32[]{:S(2)}, u32[]{:S(2)}) collective-permute-start(bf16[1,128,512]{2,1,0:T(8,128)(2,1)S(1)} %get-tuple-element.111), channel_id=1, source_target_pairs={{0,8},{8,16},{16,24},{1,9},{9,17},{17,25},{2,10},{10,18},{18,26},{... | collective-permute-start | bytes 393224 | tf_op jit(solution)/shard_map/ppermute | solution.py:10
  259.8 0.7 copy-start.26
  260.5 79.1 %all-gather.33.cloned.1.call-start = ((), (), s32[]{:S(2)}) async-start(), calls=%async_computation.9 | async-start | bytes 1179648 | tf_op jit(solution)/shard_map/while/body/eval_jaxpr/all_gather | solution.py:39
  283.5 33.9 %copy-start.15 = (f32[1,128,512]{2,1,0:T(8,128)S(1)}, f32[1,128,512]{2,1,0:T(8,128)}, u32[]{:S(2)}) copy-start(f32[1,128,512]{2,1,0:T(8,128)} %get-tuple-element.122) | copy-start | bytes 786436
  314.7 0.7 copy-start.17
  317.3 45.8 %all-gather.31.cloned.1.call-start = ((), (), s32[]{:S(2)}) async-start(), calls=%async_computation.8 | async-start | bytes 1179648 | tf_op jit(solution)/shard_map/all_gather | solution.py:65
  319.4 7.7 %copy-start.8 = (bf16[4,128,512]{2,1,0:T(8,128)(2,1)}, bf16[4,128,512]{2,1,0:T(8,128)(2,1)S(1)}, u32[]{:S(2)}) copy-start(bf16[4,128,512]{2,1,0:T(8,128)(2,1)S(1)} %get-tuple-element.98) | copy-start | bytes 1572868
  319.4 6.8 %collective-permute-start.4 = (bf16[1,128,512]{2,1,0:T(8,128)(2,1)S(1)}, bf16[1,128,512]{2,1,0:T(8,128)(2,1)S(1)}, u32[]{:S(2)}, u32[]{:S(2)}) collective-permute-start(bf16[1,128,512]{2,1,0:T(8,128)(2,1)S(1)} %get-tuple-element.99), channel_id=1, source_target_pairs={{0,8},{8,16},{16,24},{1,9},{9,17},{17,25},{2,10},{10,18},{18,26},{... | collective-permute-start | bytes 393224 | tf_op jit(solution)/shard_map/ppermute | solution.py:10
  326.2 0.7 copy-start.22
  326.9 77.8 %all-gather.37.cloned.1.call-start = ((), (), s32[]{:S(2)}) async-start(), calls=%async_computation.11 | async-start | bytes 1179648 | tf_op jit(solution)/shard_map/while/body/eval_jaxpr/all_gather | solution.py:39
  350.1 30.3 %copy-start.2 = (f32[128,1,512]{2,0,1:T(8,128)S(1)}, f32[128,1,512]{2,0,1:T(8,128)}, u32[]{:S(2)}) copy-start(f32[128,1,512]{2,0,1:T(8,128)} %copy-done.1) | copy-start | bytes 786436
  350.1 32.4 %copy-start.9 = (bf16[4,128,512]{2,1,0:T(8,128)(2,1)S(1)}, bf16[4,128,512]{2,1,0:T(8,128)(2,1)}, u32[]{:S(2)}) copy-start(bf16[4,128,512]{2,1,0:T(8,128)(2,1)} %copy-done.8) | copy-start | bytes 1572868
  379.7 0.7 copy-start.19
  379.7 34.2 %copy-start.10 = (f32[128,1,512]{2,1,0:T(1,128)}, f32[128,1,512]{2,1,0:T(1,128)S(1)}, u32[]{:S(2)}) copy-start(f32[128,1,512]{2,1,0:T(1,128)S(1)} %get-tuple-element.156) | copy-start | bytes 786436
  379.7 34.2 %copy-start.12 = (f32[128,1,512]{2,1,0:T(1,128)}, f32[128,1,512]{2,1,0:T(1,128)S(1)}, u32[]{:S(2)}) copy-start(f32[128,1,512]{2,1,0:T(1,128)S(1)} %get-tuple-element.157) | copy-start | bytes 786436
  382.4 46.4 %all-gather.35.cloned.1.call-start = ((), (), s32[]{:S(2)}) async-start(), calls=%async_computation.10 | async-start | bytes 1179648 | tf_op jit(solution)/shard_map/all_gather | solution.py:65
  383.9 6.8 %collective-permute-start.5 = (bf16[1,128,512]{2,1,0:T(8,128)(2,1)S(1)}, bf16[1,128,512]{2,1,0:T(8,128)(2,1)S(1)}, u32[]{:S(2)}, u32[]{:S(2)}) collective-permute-start(bf16[1,128,512]{2,1,0:T(8,128)(2,1)S(1)} %get-tuple-element.89), channel_id=1, source_target_pairs={{0,8},{8,16},{16,24},{1,9},{9,17},{17,25},{2,10},{10,18},{18,26},{... | collective-permute-start | bytes 393224 | tf_op jit(solution)/shard_map/ppermute | solution.py:10
  390.7 0.7 copy-start.21
  413.9 29.0 %copy-start.16 = (f32[1,128,512]{2,1,0:T(8,128)S(1)}, f32[1,128,512]{2,1,0:T(8,128)}, u32[]{:S(2)}) copy-start(f32[1,128,512]{2,1,0:T(8,128)} %get-tuple-element.100) | copy-start | bytes 786436
  428.8 14.1 %copy-start.11 = (f32[128,1,512]{2,1,0:T(1,128)S(1)}, f32[128,1,512]{2,1,0:T(1,128)}, u32[]{:S(2)}) copy-start(f32[128,1,512]{2,1,0:T(1,128)} %copy-done.10) | copy-start | bytes 786436
  428.8 14.1 %copy-start.13 = (f32[128,1,512]{2,1,0:T(1,128)S(1)}, f32[128,1,512]{2,1,0:T(1,128)}, u32[]{:S(2)}) copy-start(f32[128,1,512]{2,1,0:T(1,128)} %copy-done.12) | copy-start | bytes 786436
Sparse Core Ops, SparseCore 0:
  9.6 24.9 all-gather.38
  55.9 24.8 all-gather.16
  83.0 21.8 all-gather.14
  122.2 22.3 all-gather.20
  146.0 21.8 all-gather.18
  187.3 22.1 all-gather.24
  211.1 21.8 all-gather.22
  251.8 22.1 all-gather.28
  276.2 21.8 all-gather.26
  317.4 22.1 all-gather.32
  341.3 21.8 all-gather.30
  382.5 22.1 all-gather.36
  406.9 21.8 all-gather.34
where the time goes:
time: 459 us; the launch traced here: 452 us
  waiting for transfers between devices  183 us (40%)
  matrix products  129 us (28%)
  local copies, waits for them, and re-layouts  75.9 us (17%)
  starting transfers between devices  25.3 us (6%)
  other arithmetic  23.8 us (5%)
  between operations  14.6 us (3%)
    all_gather x6, waiting for transfers between devices, body(): arrived = lax.all_gather(received, 'col', axis=2, tiled=True)  82.4 us
    all_gather x6, waiting for transfers between devices, advance(): hidden_wide = lax.all_gather(hidden_new, 'col', axis=1, tiled=True)  81.2 us
    dot_general x7, matrix products, body(): jnp.dot(source.reshape(span * batch, width), weight_in, preferred_element...  65.6 us
    dot_general x7, matrix products, advance(): jnp.dot(hidden_prev, weight_rec, preferred_element_type=jnp.float32)  63.8 us
    unnamed x58, local copies, waits for them, and re-layouts  35.2 us
    ppermute x6, starting transfers between devices, passed_along(): lax.ppermute(value, axis, [(source, source + steps) for source in range(f...  23.5 us
    ppermute x6, waiting for transfers between devices, passed_along(): lax.ppermute(value, axis, [(source, source + steps) for source in range(f...  18.1 us
    reshape x7, local copies, waits for them, and re-layouts, advance(): gates = gates.reshape(batch, 4, local)  17 us
  transfers between devices with their start and end apart: 19, of which 18 were waited for; matrix products, arithmetic and copies ran while one was open for 23% of the time, Pallas kernels for 0%

commit v1 on v0

--- a/solution.py
+++ b/solution.py
@@ -36,7 +36,14 @@
             gates[:, 2]
         )
         hidden_new = (jax.nn.sigmoid(gates[:, 3]) * jnp.tanh(cell_new)).astype(jnp.bfloat16)
-        hidden_wide = lax.all_gather(hidden_new, "col", axis=1, tiled=True)
+        ring = [hidden_new]
+        for hop in range(7):
+            ring.append(lax.ppermute(ring[-1], "col", [(dev, (dev + 1) % 8) for dev in range(8)]))
+        hidden_wide = jnp.roll(
+            jnp.concatenate(ring[::-1], axis=1),
+            (lax.axis_index("col") + 1) * ring[0].shape[1],
+            axis=1,
+        )
         return ((hidden_wide, cell_new), (hidden_new, hidden_wide))
 
     for turn in range(rounds):

time: 459 us -> 552 us (1.20)
  waiting for transfers between devices: 183 us -> 262 us
  local copies, waits for them, and re-layouts: 75.9 us -> 89.2 us
    ppermute x0 -> x42, waiting for transfers between devices: none -> 220 us  [advance(): lax.ppermute(ring[-1], 'col', [(dev, (dev + 1) % 8) for dev in range(8)])]
    all_gather x6 -> x0, waiting for transfers between devices: 81.2 us -> none  [advance(): hidden_wide = lax.all_gather(hidden_new, 'col', axis=1, tiled=True)]
    all_gather x6, waiting for transfers between devices: 82.4 us -> 34.8 us  [body(): arrived = lax.all_gather(received, 'col', axis=2, tiled=True)]
    unnamed x58 -> x110, local copies, waits for them, and re-layouts: 35.2 us -> 53.6 us
    ppermute x6, waiting for transfers between devices: 18.1 us -> 5.97 us  [passed_along(): lax.ppermute(value, axis, [(source, source + steps) for source in range(f...]
  transfers between devices with their start and end apart: 19 -> 55, of which waited for: 18 -> 52; matrix products, arithmetic and copies ran while one was open for 23% -> 22% of each run, Pallas kernels for 0% -> 0%
where the time goes in v1:
time: 552 us; the launch traced here: 544 us
  waiting for transfers between devices  262 us (47%)
  matrix products  129 us (23%)
  local copies, waits for them, and re-layouts  89.2 us (16%)
  starting transfers between devices  26.7 us (5%)
  other arithmetic  22.2 us (4%)
  between operations  15.4 us (3%)
    ppermute x42, waiting for transfers between devices, advance(): lax.ppermute(ring[-1], 'col', [(dev, (dev + 1) % 8) for dev in range(8)])  220 us
    dot_general x7, matrix products, body(): jnp.dot(source.reshape(span * batch, width), weight_in, preferred_element...  65.3 us
    dot_general x7, matrix products, advance(): jnp.dot(hidden_prev, weight_rec, preferred_element_type=jnp.float32)  63.3 us
    unnamed x110, local copies, waits for them, and re-layouts  53.6 us
    all_gather x6, waiting for transfers between devices, body(): arrived = lax.all_gather(received, 'col', axis=2, tiled=True)  34.8 us
    ppermute x6, starting transfers between devices, passed_along(): lax.ppermute(value, axis, [(source, source + steps) for source in range(f...  23 us
    reshape x7, local copies, waits for them, and re-layouts, advance(): gates = gates.reshape(batch, 4, local)  16 us
    slice x5, local copies, waits for them, and re-layouts, advance(): gates[:, 0]  15.2 us
  transfers between devices with their start and end apart: 55, of which 52 were waited for; matrix products, arithmetic and copies ran while one was open for 22% of the time, Pallas kernels for 0%

profile of v1, /device:TPU:0, one launch (start us, length us, event | category | flops | bytes accessed | tf_op | source)
XLA Modules:
  0.0 544.0 jit_solution(10443811419673792942)
XLA Ops:
  8.0 18.1 %copy.64 = bf16[512,8,4,512]{3,1,2,0:T(8,128)(2,1)} copy(bf16[512,8,4,512]{3,2,1,0:T(4,128)(2,1)} %bitcast.367) | data formatting | bytes 33554432
  26.1 9.4 %copy.66 = bf16[512,8,4,512]{3,1,2,0:T(8,128)(2,1)} copy(bf16[512,8,4,512]{3,2,1,0:T(4,128)(2,1)S(1)} %bitcast.368) | data formatting | bytes 33554432
  35.5 8.4 %convolution_add_fusion.7 = f32[128,2048]{1,0:T(8,128)S(1)} fusion(bf16[4096,2048]{1,0:T(8,128)(2,1)} %bitcast.353, bf16[4,128,4096]{2,1,0:T(8,128)(2,1)} %param.8, s32[]{:T(128)S(6)} %min.22, pred[]{:T(512)S(6)} %eq.4, f32[2048]{0:T(1024)S(1)} %bitcast.370), kind=kOutput, calls=%fused_computation.13 | convolution fusion | flops 2148270080 | bytes 18882564 | tf_op jit(solution)/shard_map/dot_general | solution.py:56
  44.0 8.5 %convolution_add_fusion.6 = f32[128,2048]{1,0:T(8,128)S(1)} fusion(f32[128,2048]{1,0:T(8,128)S(1)} %convolution_add_fusion.7, bf16[4096,2048]{1,0:T(8,128)(2,1)} %bitcast.360, bf16[1,128,4096]{2,1,0:T(8,128)(2,1)} %all-gather.21.cloned.1.call-done), kind=kOutput, calls=%fused_computation.12 | convolution fusion | flops 2147745792 | bytes 19922944 | tf_op jit(solution)/shard_map/while/body/eval_jaxpr/dot_general | solution.py:33
  54.9 6.7 %collective-permute-done.1 = bf16[128,512]{1,0:T(8,128)(2,1)S(1)} collective-permute-done((bf16[128,512]{1,0:T(8,128)(2,1)S(1)}, bf16[128,512]{1,0:T(8,128)(2,1)S(1)}, u32[]{:S(2)}, u32[]{:S(2)}) %collective-permute-start.1) | collective-permute-done | bytes 131104 | tf_op jit(solution)/shard_map/while/body/eval_jaxpr/ppermute | solution.py:41
  61.6 6.2 %collective-permute-done.2 = bf16[128,512]{1,0:T(8,128)(2,1)S(1)} collective-permute-done((bf16[128,512]{1,0:T(8,128)(2,1)S(1)}, bf16[128,512]{1,0:T(8,128)(2,1)S(1)}, u32[]{:S(2)}, u32[]{:S(2)}) %collective-permute-start.2) | collective-permute-done | bytes 131104 | tf_op jit(solution)/shard_map/while/body/eval_jaxpr/ppermute | solution.py:41
  67.8 6.2 %collective-permute-done.3 = bf16[128,512]{1,0:T(8,128)(2,1)S(1)} collective-permute-done((bf16[128,512]{1,0:T(8,128)(2,1)S(1)}, bf16[128,512]{1,0:T(8,128)(2,1)S(1)}, u32[]{:S(2)}, u32[]{:S(2)}) %collective-permute-start.3) | collective-permute-done | bytes 131104 | tf_op jit(solution)/shard_map/while/body/eval_jaxpr/ppermute | solution.py:41
  74.0 6.2 %collective-permute-done.4 = bf16[128,512]{1,0:T(8,128)(2,1)S(1)} collective-permute-done((bf16[128,512]{1,0:T(8,128)(2,1)S(1)}, bf16[128,512]{1,0:T(8,128)(2,1)S(1)}, u32[]{:S(2)}, u32[]{:S(2)}) %collective-permute-start.4) | collective-permute-done | bytes 131104 | tf_op jit(solution)/shard_map/while/body/eval_jaxpr/ppermute | solution.py:41
  80.2 6.2 %collective-permute-done.5 = bf16[128,512]{1,0:T(8,128)(2,1)S(1)} collective-permute-done((bf16[128,512]{1,0:T(8,128)(2,1)S(1)}, bf16[128,512]{1,0:T(8,128)(2,1)S(1)}, u32[]{:S(2)}, u32[]{:S(2)}) %collective-permute-start.5) | collective-permute-done | bytes 131104 | tf_op jit(solution)/shard_map/while/body/eval_jaxpr/ppermute | solution.py:41
  100.8 9.3 %fusion.171 = f32[128,2048]{1,0:T(8,128)} fusion(bf16[128,4096]{1,0:T(8,128)(2,1)S(1)} %fusion.19, bf16[4096,2048]{1,0:T(8,128)(2,1)} %bitcast.361), kind=kOutput, calls=%fused_computation.307 | convolution fusion | flops 2147483648 | bytes 18874368 | tf_op jit(solution)/shard_map/while/body/eval_jaxpr/dot_general | solution.py:33
  110.1 7.2 %all-gather.9.cloned.1.call-done = bf16[1,128,4096]{2,1,0:T(8,128)(2,1)} async-done(((bf16[1,128,512]{2,1,0:T(8,128)(2,1)}), bf16[1,128,4096]{2,1,0:T(8,128)(2,1)}) %all-gather.9.cloned.1.call-update) | async-done | bytes 1048592 | tf_op jit(solution)/shard_map/all_gather | solution.py:72
  117.3 9.7 %fusion.5 = f32[128,2048]{1,0:T(8,128)} fusion(f32[128,2048]{1,0:T(8,128)} %fusion.171, bf16[4096,2048]{1,0:T(8,128)(2,1)} %bitcast.354, bf16[1,128,4096]{2,1,0:T(8,128)(2,1)} %all-gather.9.cloned.1.call-done, bf16[4,128,4096]{2,1,0:T(8,128)(2,1)} %param.8, s32[]{:T(128)S(6)} %min.23, pred[]{:T(512)S(6)} %eq.4, f32[2048]{0:T(1024)S(1)} %bitcast.371), kind=kOutput, calls=%fused_computation.11 | convolution fusion | flops 2148532224 | bytes 20979716 | tf_op jit(solution)/shard_map/dot_general | solution.py:56
  140.8 6.2 %collective-permute-done.10 = bf16[128,512]{1,0:T(8,128)(2,1)S(1)} collective-permute-done((bf16[128,512]{1,0:T(8,128)(2,1)S(1)}, bf16[128,512]{1,0:T(8,128)(2,1)S(1)}, u32[]{:S(2)}, u32[]{:S(2)}) %collective-permute-start.10) | collective-permute-done | bytes 131104 | tf_op jit(solution)/shard_map/while/body/eval_jaxpr/ppermute | solution.py:41
  146.9 6.2 %collective-permute-done.11 = bf16[128,512]{1,0:T(8,128)(2,1)S(1)} collective-permute-done((bf16[128,512]{1,0:T(8,128)(2,1)S(1)}, bf16[128,512]{1,0:T(8,128)(2,1)S(1)}, u32[]{:S(2)}, u32[]{:S(2)}) %collective-permute-start.11) | collective-permute-done | bytes 131104 | tf_op jit(solution)/shard_map/while/body/eval_jaxpr/ppermute | solution.py:41
  153.8 6.3 %collective-permute-done.12 = bf16[128,512]{1,0:T(8,128)(2,1)} collective-permute-done((bf16[128,512]{1,0:T(8,128)(2,1)S(1)}, bf16[128,512]{1,0:T(8,128)(2,1)}, u32[]{:S(2)}, u32[]{:S(2)}) %collective-permute-start.12) | collective-permute-done | bytes 131104 | tf_op jit(solution)/shard_map/while/body/eval_jaxpr/ppermute | solution.py:41
  160.1 6.5 %collective-permute-done.13 = bf16[128,512]{1,0:T(8,128)(2,1)} collective-permute-done((bf16[128,512]{1,0:T(8,128)(2,1)}, bf16[128,512]{1,0:T(8,128)(2,1)}, u32[]{:S(2)}, u32[]{:S(2)}) %collective-permute-start.13) | collective-permute-done | bytes 131104 | tf_op jit(solution)/shard_map/while/body/eval_jaxpr/ppermute | solution.py:41
  184.8 8.2 %fusion.172 = f32[128,2048]{1,0:T(8,128)S(1)} fusion(bf16[128,4096]{1,0:T(8,128)(2,1)S(1)} %fusion.17, bf16[4096,2048]{1,0:T(8,128)(2,1)} %bitcast.362), kind=kOutput, calls=%fused_computation.308 | convolution fusion | flops 2147483648 | bytes 18874368 | tf_op jit(solution)/shard_map/while/body/eval_jaxpr/dot_general | solution.py:33
  197.6 9.5 %fusion.4 = f32[128,2048]{1,0:T(8,128)} fusion(f32[128,2048]{1,0:T(8,128)S(1)} %fusion.172, bf16[4096,2048]{1,0:T(8,128)(2,1)} %bitcast.355, bf16[1,128,4096]{2,1,0:T(8,128)(2,1)} %all-gather.11.cloned.1.call-done, bf16[4,128,4096]{2,1,0:T(8,128)(2,1)} %param.8, s32[]{:T(128)S(6)} %min.24, pred[]{:T(512)S(6)} %eq.4, f32[2048]{0:T(1024)S(1)} %bitcast.372), kind=kOutput, calls=%fused_computation.9 | convolution fusion | flops 2148532224 | bytes 20979716 | tf_op jit(solution)/shard_map/dot_general | solution.py:56
  215.3 6.0 %collective-permute-done.17 = bf16[128,512]{1,0:T(8,128)(2,1)S(1)} collective-permute-done((bf16[128,512]{1,0:T(8,128)(2,1)S(1)}, bf16[128,512]{1,0:T(8,128)(2,1)S(1)}, u32[]{:S(2)}, u32[]{:S(2)}) %collective-permute-start.17) | collective-permute-done | bytes 131104 | tf_op jit(solution)/shard_map/while/body/eval_jaxpr/ppermute | solution.py:41
  221.3 6.2 %collective-permute-done.18 = bf16[128,512]{1,0:T(8,128)(2,1)S(1)} collective-permute-done((bf16[128,512]{1,0:T(8,128)(2,1)S(1)}, bf16[128,512]{1,0:T(8,128)(2,1)S(1)}, u32[]{:S(2)}, u32[]{:S(2)}) %collective-permute-start.18) | collective-permute-done | bytes 131104 | tf_op jit(solution)/shard_map/while/body/eval_jaxpr/ppermute | solution.py:41
  227.5 6.2 %collective-permute-done.19 = bf16[128,512]{1,0:T(8,128)(2,1)S(1)} collective-permute-done((bf16[128,512]{1,0:T(8,128)(2,1)S(1)}, bf16[128,512]{1,0:T(8,128)(2,1)S(1)}, u32[]{:S(2)}, u32[]{:S(2)}) %collective-permute-start.19) | collective-permute-done | bytes 131104 | tf_op jit(solution)/shard_map/while/body/eval_jaxpr/ppermute | solution.py:41
  233.7 6.2 %collective-permute-done.20 = bf16[128,512]{1,0:T(8,128)(2,1)S(1)} collective-permute-done((bf16[128,512]{1,0:T(8,128)(2,1)S(1)}, bf16[128,512]{1,0:T(8,128)(2,1)S(1)}, u32[]{:S(2)}, u32[]{:S(2)}) %collective-permute-start.20) | collective-permute-done | bytes 131104 | tf_op jit(solution)/shard_map/while/body/eval_jaxpr/ppermute | solution.py:41
  239.9 6.3 %collective-permute-done.21 = bf16[128,512]{1,0:T(8,128)(2,1)} collective-permute-done((bf16[128,512]{1,0:T(8,128)(2,1)S(1)}, bf16[128,512]{1,0:T(8,128)(2,1)}, u32[]{:S(2)}, u32[]{:S(2)}) %collective-permute-start.21) | collective-permute-done | bytes 131104 | tf_op jit(solution)/shard_map/while/body/eval_jaxpr/ppermute | solution.py:41
  262.6 9.3 %fusion.173 = f32[128,2048]{1,0:T(8,128)} fusion(bf16[128,4096]{1,0:T(8,128)(2,1)S(1)} %fusion.15, bf16[4096,2048]{1,0:T(8,128)(2,1)} %bitcast.363), kind=kOutput, calls=%fused_computation.309 | convolution fusion | flops 2147483648 | bytes 18874368 | tf_op jit(solution)/shard_map/while/body/eval_jaxpr/dot_general | solution.py:33
  271.8 6.7 %all-gather.13.cloned.1.call-done = bf16[1,128,4096]{2,1,0:T(8,128)(2,1)} async-done(((bf16[1,128,512]{2,1,0:T(8,128)(2,1)}), bf16[1,128,4096]{2,1,0:T(8,128)(2,1)}) %all-gather.13.cloned.1.call-update) | async-done | bytes 1048592 | tf_op jit(solution)/shard_map/all_gather | solution.py:72
  278.5 9.7 %fusion.3 = f32[128,2048]{1,0:T(8,128)} fusion(f32[128,2048]{1,0:T(8,128)} %fusion.173, bf16[4096,2048]{1,0:T(8,128)(2,1)} %bitcast.356, bf16[1,128,4096]{2,1,0:T(8,128)(2,1)} %all-gather.13.cloned.1.call-done, bf16[4,128,4096]{2,1,0:T(8,128)(2,1)} %param.8, s32[]{:T(128)S(6)} %min.25, pred[]{:T(512)S(6)} %eq.4, f32[2048]{0:T(1024)S(1)} %bitcast.373), kind=kOutput, calls=%fused_computation.7 | convolution fusion | flops 2148532224 | bytes 20979716 | tf_op jit(solution)/shard_map/dot_general | solution.py:56
  296.1 6.0 %collective-permute-done.25 = bf16[128,512]{1,0:T(8,128)(2,1)S(1)} collective-permute-done((bf16[128,512]{1,0:T(8,128)(2,1)S(1)}, bf16[128,512]{1,0:T(8,128)(2,1)S(1)}, u32[]{:S(2)}, u32[]{:S(2)}) %collective-permute-start.25) | collective-permute-done | bytes 131104 | tf_op jit(solution)/shard_map/while/body/eval_jaxpr/ppermute | solution.py:41
  302.0 6.2 %collective-permute-done.26 = bf16[128,512]{1,0:T(8,128)(2,1)S(1)} collective-permute-done((bf16[128,512]{1,0:T(8,128)(2,1)S(1)}, bf16[128,512]{1,0:T(8,128)(2,1)S(1)}, u32[]{:S(2)}, u32[]{:S(2)}) %collective-permute-start.26) | collective-permute-done | bytes 131104 | tf_op jit(solution)/shard_map/while/body/eval_jaxpr/ppermute | solution.py:41
  308.2 6.2 %collective-permute-done.27 = bf16[128,512]{1,0:T(8,128)(2,1)S(1)} collective-permute-done((bf16[128,512]{1,0:T(8,128)(2,1)S(1)}, bf16[128,512]{1,0:T(8,128)(2,1)S(1)}, u32[]{:S(2)}, u32[]{:S(2)}) %collective-permute-start.27) | collective-permute-done | bytes 131104 | tf_op jit(solution)/shard_map/while/body/eval_jaxpr/ppermute | solution.py:41
  314.4 6.2 %collective-permute-done.28 = bf16[128,512]{1,0:T(8,128)(2,1)S(1)} collective-permute-done((bf16[128,512]{1,0:T(8,128)(2,1)S(1)}, bf16[128,512]{1,0:T(8,128)(2,1)S(1)}, u32[]{:S(2)}, u32[]{:S(2)}) %collective-permute-start.28) | collective-permute-done | bytes 131104 | tf_op jit(solution)/shard_map/while/body/eval_jaxpr/ppermute | solution.py:41
  320.6 6.2 %collective-permute-done.29 = bf16[128,512]{1,0:T(8,128)(2,1)S(1)} collective-permute-done((bf16[128,512]{1,0:T(8,128)(2,1)S(1)}, bf16[128,512]{1,0:T(8,128)(2,1)S(1)}, u32[]{:S(2)}, u32[]{:S(2)}) %collective-permute-start.29) | collective-permute-done | bytes 131104 | tf_op jit(solution)/shard_map/while/body/eval_jaxpr/ppermute | solution.py:41
  341.2 9.3 %fusion.174 = f32[128,2048]{1,0:T(8,128)} fusion(bf16[128,4096]{1,0:T(8,128)(2,1)S(1)} %fusion.13, bf16[4096,2048]{1,0:T(8,128)(2,1)} %bitcast.364), kind=kOutput, calls=%fused_computation.310 | convolution fusion | flops 2147483648 | bytes 18874368 | tf_op jit(solution)/shard_map/while/body/eval_jaxpr/dot_general | solution.py:33
  350.5 8.3 %all-gather.15.cloned.1.call-done = bf16[1,128,4096]{2,1,0:T(8,128)(2,1)} async-done(((bf16[1,128,512]{2,1,0:T(8,128)(2,1)}), bf16[1,128,4096]{2,1,0:T(8,128)(2,1)}) %all-gather.15.cloned.1.call-update) | async-done | bytes 1048592 | tf_op jit(solution)/shard_map/all_gather | solution.py:72
  358.9 9.7 %fusion.2 = f32[128,2048]{1,0:T(8,128)} fusion(f32[128,2048]{1,0:T(8,128)} %fusion.174, bf16[4096,2048]{1,0:T(8,128)(2,1)} %bitcast.357, bf16[1,128,4096]{2,1,0:T(8,128)(2,1)} %all-gather.15.cloned.1.call-done, bf16[4,128,4096]{2,1,0:T(8,128)(2,1)} %param.8, s32[]{:T(128)S(6)} %min.26, pred[]{:T(512)S(6)} %eq.4, f32[2048]{0:T(1024)S(1)} %bitcast.374), kind=kOutput, calls=%fused_computation.5 | convolution fusion | flops 2148532224 | bytes 20979716 | tf_op jit(solution)/shard_map/dot_general | solution.py:56
  377.3 6.0 %collective-permute-done.33 = bf16[128,512]{1,0:T(8,128)(2,1)S(1)} collective-permute-done((bf16[128,512]{1,0:T(8,128)(2,1)S(1)}, bf16[128,512]{1,0:T(8,128)(2,1)S(1)}, u32[]{:S(2)}, u32[]{:S(2)}) %collective-permute-start.33) | collective-permute-done | bytes 131104 | tf_op jit(solution)/shard_map/while/body/eval_jaxpr/ppermute | solution.py:41
  384.0 6.2 %collective-permute-done.34 = bf16[128,512]{1,0:T(8,128)(2,1)S(1)} collective-permute-done((bf16[128,512]{1,0:T(8,128)(2,1)S(1)}, bf16[128,512]{1,0:T(8,128)(2,1)S(1)}, u32[]{:S(2)}, u32[]{:S(2)}) %collective-permute-start.34) | collective-permute-done | bytes 131104 | tf_op jit(solution)/shard_map/while/body/eval_jaxpr/ppermute | solution.py:41
  390.8 6.2 %collective-permute-done.35 = bf16[128,512]{1,0:T(8,128)(2,1)S(1)} collective-permute-done((bf16[128,512]{1,0:T(8,128)(2,1)S(1)}, bf16[128,512]{1,0:T(8,128)(2,1)S(1)}, u32[]{:S(2)}, u32[]{:S(2)}) %collective-permute-start.35) | collective-permute-done | bytes 131104 | tf_op jit(solution)/shard_map/while/body/eval_jaxpr/ppermute | solution.py:41
  397.7 6.3 %collective-permute-done.36 = bf16[128,512]{1,0:T(8,128)(2,1)} collective-permute-done((bf16[128,512]{1,0:T(8,128)(2,1)S(1)}, bf16[128,512]{1,0:T(8,128)(2,1)}, u32[]{:S(2)}, u32[]{:S(2)}) %collective-permute-start.36) | collective-permute-done | bytes 131104 | tf_op jit(solution)/shard_map/while/body/eval_jaxpr/ppermute | solution.py:41
  404.0 6.5 %collective-permute-done.37 = bf16[128,512]{1,0:T(8,128)(2,1)} collective-permute-done((bf16[128,512]{1,0:T(8,128)(2,1)}, bf16[128,512]{1,0:T(8,128)(2,1)}, u32[]{:S(2)}, u32[]{:S(2)}) %collective-permute-start.37) | collective-permute-done | bytes 131104 | tf_op jit(solution)/shard_map/while/body/eval_jaxpr/ppermute | solution.py:41
  430.6 9.2 %fusion.175 = f32[128,2048]{1,0:T(8,128)} fusion(bf16[128,4096]{1,0:T(8,128)(2,1)S(1)} %fusion.11, bf16[4096,2048]{1,0:T(8,128)(2,1)} %bitcast.365), kind=kOutput, calls=%fused_computation.311 | convolution fusion | flops 2147483648 | bytes 18874368 | tf_op jit(solution)/shard_map/while/body/eval_jaxpr/dot_general | solution.py:33
  442.9 9.7 %fusion.1 = f32[128,2048]{1,0:T(8,128)} fusion(f32[128,2048]{1,0:T(8,128)} %fusion.175, bf16[4096,2048]{1,0:T(8,128)(2,1)} %bitcast.358, bf16[1,128,4096]{2,1,0:T(8,128)(2,1)} %all-gather.17.cloned.1.call-done, bf16[4,128,4096]{2,1,0:T(8,128)(2,1)} %param.8, s32[]{:T(128)S(6)} %min.27, pred[]{:T(512)S(6)} %eq.4, f32[2048]{0:T(1024)S(1)} %bitcast.375), kind=kOutput, calls=%fused_computation.3 | convolution fusion | flops 2148532224 | bytes 20979716 | tf_op jit(solution)/shard_map/dot_general | solution.py:56
  461.1 6.0 %collective-permute-done.41 = bf16[128,512]{1,0:T(8,128)(2,1)S(1)} collective-permute-done((bf16[128,512]{1,0:T(8,128)(2,1)S(1)}, bf16[128,512]{1,0:T(8,128)(2,1)S(1)}, u32[]{:S(2)}, u32[]{:S(2)}) %collective-permute-start.41) | collective-permute-done | bytes 131104 | tf_op jit(solution)/shard_map/while/body/eval_jaxpr/ppermute | solution.py:41
  467.1 6.2 %collective-permute-done.42 = bf16[128,512]{1,0:T(8,128)(2,1)S(1)} collective-permute-done((bf16[128,512]{1,0:T(8,128)(2,1)S(1)}, bf16[128,512]{1,0:T(8,128)(2,1)S(1)}, u32[]{:S(2)}, u32[]{:S(2)}) %collective-permute-start.42) | collective-permute-done | bytes 131104 | tf_op jit(solution)/shard_map/while/body/eval_jaxpr/ppermute | solution.py:41
  473.3 6.2 %collective-permute-done.43 = bf16[128,512]{1,0:T(8,128)(2,1)S(1)} collective-permute-done((bf16[128,512]{1,0:T(8,128)(2,1)S(1)}, bf16[128,512]{1,0:T(8,128)(2,1)S(1)}, u32[]{:S(2)}, u32[]{:S(2)}) %collective-permute-start.43) | collective-permute-done | bytes 131104 | tf_op jit(solution)/shard_map/while/body/eval_jaxpr/ppermute | solution.py:41
  479.4 6.2 %collective-permute-done.44 = bf16[128,512]{1,0:T(8,128)(2,1)S(1)} collective-permute-done((bf16[128,512]{1,0:T(8,128)(2,1)S(1)}, bf16[128,512]{1,0:T(8,128)(2,1)S(1)}, u32[]{:S(2)}, u32[]{:S(2)}) %collective-permute-start.44) | collective-permute-done | bytes 131104 | tf_op jit(solution)/shard_map/while/body/eval_jaxpr/ppermute | solution.py:41
  485.6 6.3 %collective-permute-done.45 = bf16[128,512]{1,0:T(8,128)(2,1)} collective-permute-done((bf16[128,512]{1,0:T(8,128)(2,1)S(1)}, bf16[128,512]{1,0:T(8,128)(2,1)}, u32[]{:S(2)}, u32[]{:S(2)}) %collective-permute-start.45) | collective-permute-done | bytes 131104 | tf_op jit(solution)/shard_map/while/body/eval_jaxpr/ppermute | solution.py:41
  509.0 9.5 %fusion.8 = f32[128,2048]{1,0:T(8,128)} fusion(bf16[4096,2048]{1,0:T(8,128)(2,1)} %bitcast.366, bf16[128,4096]{1,0:T(8,128)(2,1)S(1)} %copy-done.9, s32[]{:T(128)S(6)} %select_n.320, bf16[128,4096]{1,0:T(8,128)(2,1)S(1)} %constant_dynamic-update-slice_fusion.40, pred[]{:T(512)S(6)} %and.33), kind=kOutput, calls=%fused_computation.28 | convolution fusion | flops 2150105088 | bytes 19922948 | tf_op jit(solution)/shard_map/while/body/eval_jaxpr/dot_general | solution.py:33
  523.4 8.7 %fusion = f32[128,2048]{1,0:T(8,128)S(1)} fusion(f32[128,2048]{1,0:T(8,128)} %fusion.8, bf16[4096,2048]{1,0:T(8,128)(2,1)} %bitcast.359, bf16[1,128,4096]{2,1,0:T(8,128)(2,1)} %all-gather.19.cloned.1.call-done, bf16[4,128,4096]{2,1,0:T(8,128)(2,1)} %param.8, s32[]{:T(128)S(6)} %min.28, pred[]{:T(512)S(6)} %eq.4, f32[2048]{0:T(1024)S(1)} %bitcast.376), kind=kOutput, calls=%fused_computation.1 | convolution fusion | flops 2148532224 | bytes 20979716 | tf_op jit(solution)/shard_map/dot_general | solution.py:56
  (233 shorter events, 170.1 us)
Async XLA Ops:
  7.2 36.8 %all-gather.21.cloned.1.call-start = ((), (), s32[]{:S(2)}) async-start(), calls=%async_computation.6 | async-start | bytes 1179648 | tf_op jit(solution)/shard_map/all_gather | solution.py:26
  7.9 109.4 %all-gather.9.cloned.1.call-start = ((), (), s32[]{:S(2)}) async-start(), calls=%async_computation | async-start | bytes 1179648 | tf_op jit(solution)/shard_map/all_gather | solution.py:72
  54.3 7.3 %collective-permute-start.1 = (bf16[128,512]{1,0:T(8,128)(2,1)S(1)}, bf16[128,512]{1,0:T(8,128)(2,1)S(1)}, u32[]{:S(2)}, u32[]{:S(2)}) collective-permute-start(bf16[128,512]{1,0:T(8,128)(2,1)S(1)} %get-tuple-element.135), channel_id=1, source_target_pairs={{0,1},{1,2},{2,3},{3,4},{4,5},{5,6},{6,7},{7,0},{8,9},{9,10},{10,1... | collective-permute-start | bytes 393224 | tf_op jit(solution)/shard_map/while/body/eval_jaxpr/ppermute | solution.py:41
  61.6 6.2 %collective-permute-start.2 = (bf16[128,512]{1,0:T(8,128)(2,1)S(1)}, bf16[128,512]{1,0:T(8,128)(2,1)S(1)}, u32[]{:S(2)}, u32[]{:S(2)}) collective-permute-start(bf16[128,512]{1,0:T(8,128)(2,1)S(1)} %collective-permute-done.1), channel_id=1, source_target_pairs={{0,1},{1,2},{2,3},{3,4},{4,5},{5,6},{6,7},{7,0},{8,9},{9,10},{10,1... | collective-permute-start | bytes 393224 | tf_op jit(solution)/shard_map/while/body/eval_jaxpr/ppermute | solution.py:41
  67.8 6.2 %collective-permute-start.3 = (bf16[128,512]{1,0:T(8,128)(2,1)S(1)}, bf16[128,512]{1,0:T(8,128)(2,1)S(1)}, u32[]{:S(2)}, u32[]{:S(2)}) collective-permute-start(bf16[128,512]{1,0:T(8,128)(2,1)S(1)} %collective-permute-done.2), channel_id=1, source_target_pairs={{0,1},{1,2},{2,3},{3,4},{4,5},{5,6},{6,7},{7,0},{8,9},{9,10},{10,1... | collective-permute-start | bytes 393224 | tf_op jit(solution)/shard_map/while/body/eval_jaxpr/ppermute | solution.py:41
  74.0 6.2 %collective-permute-start.4 = (bf16[128,512]{1,0:T(8,128)(2,1)S(1)}, bf16[128,512]{1,0:T(8,128)(2,1)S(1)}, u32[]{:S(2)}, u32[]{:S(2)}) collective-permute-start(bf16[128,512]{1,0:T(8,128)(2,1)S(1)} %collective-permute-done.3), channel_id=1, source_target_pairs={{0,1},{1,2},{2,3},{3,4},{4,5},{5,6},{6,7},{7,0},{8,9},{9,10},{10,1... | collective-permute-start | bytes 393224 | tf_op jit(solution)/shard_map/while/body/eval_jaxpr/ppermute | solution.py:41
  80.1 6.2 %collective-permute-start.5 = (bf16[128,512]{1,0:T(8,128)(2,1)S(1)}, bf16[128,512]{1,0:T(8,128)(2,1)S(1)}, u32[]{:S(2)}, u32[]{:S(2)}) collective-permute-start(bf16[128,512]{1,0:T(8,128)(2,1)S(1)} %collective-permute-done.4), channel_id=1, source_target_pairs={{0,1},{1,2},{2,3},{3,4},{4,5},{5,6},{6,7},{7,0},{8,9},{9,10},{10,1... | collective-permute-start | bytes 393224 | tf_op jit(solution)/shard_map/while/body/eval_jaxpr/ppermute | solution.py:41
  86.3 6.2 %collective-permute-start.6 = (bf16[128,512]{1,0:T(8,128)(2,1)S(1)}, bf16[128,512]{1,0:T(8,128)(2,1)S(1)}, u32[]{:S(2)}, u32[]{:S(2)}) collective-permute-start(bf16[128,512]{1,0:T(8,128)(2,1)S(1)} %collective-permute-done.5), channel_id=1, source_target_pairs={{0,1},{1,2},{2,3},{3,4},{4,5},{5,6},{6,7},{7,0},{8,9},{9,10},{10,1... | collective-permute-start | bytes 393224 | tf_op jit(solution)/shard_map/while/body/eval_jaxpr/ppermute | solution.py:41
  86.6 6.4 %collective-permute-start = (bf16[1,128,512]{2,1,0:T(8,128)(2,1)S(1)}, bf16[1,128,512]{2,1,0:T(8,128)(2,1)S(1)}, u32[]{:S(2)}, u32[]{:S(2)}) collective-permute-start(bf16[1,128,512]{2,1,0:T(8,128)(2,1)S(1)} %get-tuple-element.144), channel_id=1, source_target_pairs={{0,8},{8,16},{16,24},{1,9},{9,17},{17,25},{2,10},{10,18},{18,26},{... | collective-permute-start | bytes 393224 | tf_op jit(solution)/shard_map/ppermute | solution.py:10
  92.5 6.2 %collective-permute-start.7 = (bf16[128,512]{1,0:T(8,128)(2,1)S(1)}, bf16[128,512]{1,0:T(8,128)(2,1)S(1)}, u32[]{:S(2)}, u32[]{:S(2)}) collective-permute-start(bf16[128,512]{1,0:T(8,128)(2,1)S(1)} %collective-permute-done.6), channel_id=1, source_target_pairs={{0,1},{1,2},{2,3},{3,4},{4,5},{5,6},{6,7},{7,0},{8,9},{9,10},{10,1... | collective-permute-start | bytes 393224 | tf_op jit(solution)/shard_map/while/body/eval_jaxpr/ppermute | solution.py:41
  93.7 104.0 %all-gather.11.cloned.1.call-start = ((), (), s32[]{:S(2)}) async-start(), calls=%async_computation.1 | async-start | bytes 1179648 | tf_op jit(solution)/shard_map/all_gather | solution.py:72
  134.6 6.2 %collective-permute-start.9 = (bf16[128,512]{1,0:T(8,128)(2,1)S(1)}, bf16[128,512]{1,0:T(8,128)(2,1)S(1)}, u32[]{:S(2)}, u32[]{:S(2)}) collective-permute-start(bf16[128,512]{1,0:T(8,128)(2,1)S(1)} %get-tuple-element.124), channel_id=1, source_target_pairs={{0,1},{1,2},{2,3},{3,4},{4,5},{5,6},{6,7},{7,0},{8,9},{9,10},{10,1... | collective-permute-start | bytes 393224 | tf_op jit(solution)/shard_map/while/body/eval_jaxpr/ppermute | solution.py:41
  140.8 6.2 %collective-permute-start.10 = (bf16[128,512]{1,0:T(8,128)(2,1)S(1)}, bf16[128,512]{1,0:T(8,128)(2,1)S(1)}, u32[]{:S(2)}, u32[]{:S(2)}) collective-permute-start(bf16[128,512]{1,0:T(8,128)(2,1)S(1)} %collective-permute-done.9), channel_id=1, source_target_pairs={{0,1},{1,2},{2,3},{3,4},{4,5},{5,6},{6,7},{7,0},{8,9},{9,10},{10,1... | collective-permute-start | bytes 393224 | tf_op jit(solution)/shard_map/while/body/eval_jaxpr/ppermute | solution.py:41
  146.9 6.2 %collective-permute-start.11 = (bf16[128,512]{1,0:T(8,128)(2,1)S(1)}, bf16[128,512]{1,0:T(8,128)(2,1)S(1)}, u32[]{:S(2)}, u32[]{:S(2)}) collective-permute-start(bf16[128,512]{1,0:T(8,128)(2,1)S(1)} %collective-permute-done.10), channel_id=1, source_target_pairs={{0,1},{1,2},{2,3},{3,4},{4,5},{5,6},{6,7},{7,0},{8,9},{9,10},{10,1... | collective-permute-start | bytes 393224 | tf_op jit(solution)/shard_map/while/body/eval_jaxpr/ppermute | solution.py:41
  153.8 6.3 %collective-permute-start.12 = (bf16[128,512]{1,0:T(8,128)(2,1)S(1)}, bf16[128,512]{1,0:T(8,128)(2,1)}, u32[]{:S(2)}, u32[]{:S(2)}) collective-permute-start(bf16[128,512]{1,0:T(8,128)(2,1)S(1)} %collective-permute-done.11), channel_id=1, source_target_pairs={{0,1},{1,2},{2,3},{3,4},{4,5},{5,6},{6,7},{7,0},{8,9},{9,10},{10,1... | collective-permute-start | bytes 393224 | tf_op jit(solution)/shard_map/while/body/eval_jaxpr/ppermute | solution.py:41
  160.1 6.5 %collective-permute-start.13 = (bf16[128,512]{1,0:T(8,128)(2,1)}, bf16[128,512]{1,0:T(8,128)(2,1)}, u32[]{:S(2)}, u32[]{:S(2)}) collective-permute-start(bf16[128,512]{1,0:T(8,128)(2,1)} %collective-permute-done.12), channel_id=1, source_target_pairs={{0,1},{1,2},{2,3},{3,4},{4,5},{5,6},{6,7},{7,0},{8,9},{9,10},{10,1... | collective-permute-start | bytes 393224 | tf_op jit(solution)/shard_map/while/body/eval_jaxpr/ppermute | solution.py:41
  166.6 6.5 %collective-permute-start.14 = (bf16[128,512]{1,0:T(8,128)(2,1)}, bf16[128,512]{1,0:T(8,128)(2,1)}, u32[]{:S(2)}, u32[]{:S(2)}) collective-permute-start(bf16[128,512]{1,0:T(8,128)(2,1)} %collective-permute-done.13), channel_id=1, source_target_pairs={{0,1},{1,2},{2,3},{3,4},{4,5},{5,6},{6,7},{7,0},{8,9},{9,10},{10,1... | collective-permute-start | bytes 393224 | tf_op jit(solution)/shard_map/while/body/eval_jaxpr/ppermute | solution.py:41
  166.9 6.2 %collective-permute-start.8 = (bf16[1,128,512]{2,1,0:T(8,128)(2,1)S(1)}, bf16[1,128,512]{2,1,0:T(8,128)(2,1)S(1)}, u32[]{:S(2)}, u32[]{:S(2)}) collective-permute-start(bf16[1,128,512]{2,1,0:T(8,128)(2,1)S(1)} %get-tuple-element.134), channel_id=1, source_target_pairs={{0,8},{8,16},{16,24},{1,9},{9,17},{17,25},{2,10},{10,18},{18,26},{... | collective-permute-start | bytes 393224 | tf_op jit(solution)/shard_map/ppermute | solution.py:10
  173.1 6.4 %collective-permute-start.15 = (bf16[128,512]{1,0:T(8,128)(2,1)}, bf16[128,512]{1,0:T(8,128)(2,1)S(1)}, u32[]{:S(2)}, u32[]{:S(2)}) collective-permute-start(bf16[128,512]{1,0:T(8,128)(2,1)} %collective-permute-done.14), channel_id=1, source_target_pairs={{0,1},{1,2},{2,3},{3,4},{4,5},{5,6},{6,7},{7,0},{8,9},{9,10},{10,1... | collective-permute-start | bytes 393224 | tf_op jit(solution)/shard_map/while/body/eval_jaxpr/ppermute | solution.py:41
  173.8 104.7 %all-gather.13.cloned.1.call-start = ((), (), s32[]{:S(2)}) async-start(), calls=%async_computation.2 | async-start | bytes 1179648 | tf_op jit(solution)/shard_map/all_gather | solution.py:72
  215.0 6.2 %collective-permute-start.17 = (bf16[128,512]{1,0:T(8,128)(2,1)S(1)}, bf16[128,512]{1,0:T(8,128)(2,1)S(1)}, u32[]{:S(2)}, u32[]{:S(2)}) collective-permute-start(bf16[128,512]{1,0:T(8,128)(2,1)S(1)} %get-tuple-element.113), channel_id=1, source_target_pairs={{0,1},{1,2},{2,3},{3,4},{4,5},{5,6},{6,7},{7,0},{8,9},{9,10},{10,1... | collective-permute-start | bytes 393224 | tf_op jit(solution)/shard_map/while/body/eval_jaxpr/ppermute | solution.py:41
  221.3 6.2 %collective-permute-start.18 = (bf16[128,512]{1,0:T(8,128)(2,1)S(1)}, bf16[128,512]{1,0:T(8,128)(2,1)S(1)}, u32[]{:S(2)}, u32[]{:S(2)}) collective-permute-start(bf16[128,512]{1,0:T(8,128)(2,1)S(1)} %collective-permute-done.17), channel_id=1, source_target_pairs={{0,1},{1,2},{2,3},{3,4},{4,5},{5,6},{6,7},{7,0},{8,9},{9,10},{10,1... | collective-permute-start | bytes 393224 | tf_op jit(solution)/shard_map/while/body/eval_jaxpr/ppermute | solution.py:41
  227.5 6.2 %collective-permute-start.19 = (bf16[128,512]{1,0:T(8,128)(2,1)S(1)}, bf16[128,512]{1,0:T(8,128)(2,1)S(1)}, u32[]{:S(2)}, u32[]{:S(2)}) collective-permute-start(bf16[128,512]{1,0:T(8,128)(2,1)S(1)} %collective-permute-done.18), channel_id=1, source_target_pairs={{0,1},{1,2},{2,3},{3,4},{4,5},{5,6},{6,7},{7,0},{8,9},{9,10},{10,1... | collective-permute-start | bytes 393224 | tf_op jit(solution)/shard_map/while/body/eval_jaxpr/ppermute | solution.py:41
  233.7 6.2 %collective-permute-start.20 = (bf16[128,512]{1,0:T(8,128)(2,1)S(1)}, bf16[128,512]{1,0:T(8,128)(2,1)S(1)}, u32[]{:S(2)}, u32[]{:S(2)}) collective-permute-start(bf16[128,512]{1,0:T(8,128)(2,1)S(1)} %collective-permute-done.19), channel_id=1, source_target_pairs={{0,1},{1,2},{2,3},{3,4},{4,5},{5,6},{6,7},{7,0},{8,9},{9,10},{10,1... | collective-permute-start | bytes 393224 | tf_op jit(solution)/shard_map/while/body/eval_jaxpr/ppermute | solution.py:41
  239.8 6.3 %collective-permute-start.21 = (bf16[128,512]{1,0:T(8,128)(2,1)S(1)}, bf16[128,512]{1,0:T(8,128)(2,1)}, u32[]{:S(2)}, u32[]{:S(2)}) collective-permute-start(bf16[128,512]{1,0:T(8,128)(2,1)S(1)} %collective-permute-done.20), channel_id=1, source_target_pairs={{0,1},{1,2},{2,3},{3,4},{4,5},{5,6},{6,7},{7,0},{8,9},{9,10},{10,1... | collective-permute-start | bytes 393224 | tf_op jit(solution)/shard_map/while/body/eval_jaxpr/ppermute | solution.py:41
  246.1 6.5 %collective-permute-start.22 = (bf16[128,512]{1,0:T(8,128)(2,1)}, bf16[128,512]{1,0:T(8,128)(2,1)}, u32[]{:S(2)}, u32[]{:S(2)}) collective-permute-start(bf16[128,512]{1,0:T(8,128)(2,1)} %collective-permute-done.21), channel_id=1, source_target_pairs={{0,1},{1,2},{2,3},{3,4},{4,5},{5,6},{6,7},{7,0},{8,9},{9,10},{10,1... | collective-permute-start | bytes 393224 | tf_op jit(solution)/shard_map/while/body/eval_jaxpr/ppermute | solution.py:41
  252.7 6.4 %collective-permute-start.23 = (bf16[128,512]{1,0:T(8,128)(2,1)}, bf16[128,512]{1,0:T(8,128)(2,1)S(1)}, u32[]{:S(2)}, u32[]{:S(2)}) collective-permute-start(bf16[128,512]{1,0:T(8,128)(2,1)} %collective-permute-done.22), channel_id=1, source_target_pairs={{0,1},{1,2},{2,3},{3,4},{4,5},{5,6},{6,7},{7,0},{8,9},{9,10},{10,1... | collective-permute-start | bytes 393224 | tf_op jit(solution)/shard_map/while/body/eval_jaxpr/ppermute | solution.py:41
  255.1 103.8 %all-gather.15.cloned.1.call-start = ((), (), s32[]{:S(2)}) async-start(), calls=%async_computation.3 | async-start | bytes 1179648 | tf_op jit(solution)/shard_map/all_gather | solution.py:72
  295.8 6.2 %collective-permute-start.25 = (bf16[128,512]{1,0:T(8,128)(2,1)S(1)}, bf16[128,512]{1,0:T(8,128)(2,1)S(1)}, u32[]{:S(2)}, u32[]{:S(2)}) collective-permute-start(bf16[128,512]{1,0:T(8,128)(2,1)S(1)} %get-tuple-element.108), channel_id=1, source_target_pairs={{0,1},{1,2},{2,3},{3,4},{4,5},{5,6},{6,7},{7,0},{8,9},{9,10},{10,1... | collective-permute-start | bytes 393224 | tf_op jit(solution)/shard_map/while/body/eval_jaxpr/ppermute | solution.py:41
  302.0 6.2 %collective-permute-start.26 = (bf16[128,512]{1,0:T(8,128)(2,1)S(1)}, bf16[128,512]{1,0:T(8,128)(2,1)S(1)}, u32[]{:S(2)}, u32[]{:S(2)}) collective-permute-start(bf16[128,512]{1,0:T(8,128)(2,1)S(1)} %collective-permute-done.25), channel_id=1, source_target_pairs={{0,1},{1,2},{2,3},{3,4},{4,5},{5,6},{6,7},{7,0},{8,9},{9,10},{10,1... | collective-permute-start | bytes 393224 | tf_op jit(solution)/shard_map/while/body/eval_jaxpr/ppermute | solution.py:41
  308.2 6.2 %collective-permute-start.27 = (bf16[128,512]{1,0:T(8,128)(2,1)S(1)}, bf16[128,512]{1,0:T(8,128)(2,1)S(1)}, u32[]{:S(2)}, u32[]{:S(2)}) collective-permute-start(bf16[128,512]{1,0:T(8,128)(2,1)S(1)} %collective-permute-done.26), channel_id=1, source_target_pairs={{0,1},{1,2},{2,3},{3,4},{4,5},{5,6},{6,7},{7,0},{8,9},{9,10},{10,1... | collective-permute-start | bytes 393224 | tf_op jit(solution)/shard_map/while/body/eval_jaxpr/ppermute | solution.py:41
  326.8 6.3 %collective-permute-start.30 = (bf16[128,512]{1,0:T(8,128)(2,1)S(1)}, bf16[128,512]{1,0:T(8,128)(2,1)}, u32[]{:S(2)}, u32[]{:S(2)}) collective-permute-start(bf16[128,512]{1,0:T(8,128)(2,1)S(1)} %collective-permute-done.29), channel_id=1, source_target_pairs={{0,1},{1,2},{2,3},{3,4},{4,5},{5,6},{6,7},{7,0},{8,9},{9,10},{10,1... | collective-permute-start | bytes 393224 | tf_op jit(solution)/shard_map/while/body/eval_jaxpr/ppermute | solution.py:41
  333.1 6.4 %collective-permute-start.31 = (bf16[128,512]{1,0:T(8,128)(2,1)}, bf16[128,512]{1,0:T(8,128)(2,1)S(1)}, u32[]{:S(2)}, u32[]{:S(2)}) collective-permute-start(bf16[128,512]{1,0:T(8,128)(2,1)} %collective-permute-done.30), channel_id=1, source_target_pairs={{0,1},{1,2},{2,3},{3,4},{4,5},{5,6},{6,7},{7,0},{8,9},{9,10},{10,1... | collective-permute-start | bytes 393224 | tf_op jit(solution)/shard_map/while/body/eval_jaxpr/ppermute | solution.py:41
  335.5 107.4 %all-gather.17.cloned.1.call-start = ((), (), s32[]{:S(2)}) async-start(), calls=%async_computation.4 | async-start | bytes 1179648 | tf_op jit(solution)/shard_map/all_gather | solution.py:72
  377.1 6.2 %collective-permute-start.33 = (bf16[128,512]{1,0:T(8,128)(2,1)S(1)}, bf16[128,512]{1,0:T(8,128)(2,1)S(1)}, u32[]{:S(2)}, u32[]{:S(2)}) collective-permute-start(bf16[128,512]{1,0:T(8,128)(2,1)S(1)} %get-tuple-element.97), channel_id=1, source_target_pairs={{0,1},{1,2},{2,3},{3,4},{4,5},{5,6},{6,7},{7,0},{8,9},{9,10},{10,1... | collective-permute-start | bytes 393224 | tf_op jit(solution)/shard_map/while/body/eval_jaxpr/ppermute | solution.py:41
  384.0 6.2 %collective-permute-start.34 = (bf16[128,512]{1,0:T(8,128)(2,1)S(1)}, bf16[128,512]{1,0:T(8,128)(2,1)S(1)}, u32[]{:S(2)}, u32[]{:S(2)}) collective-permute-start(bf16[128,512]{1,0:T(8,128)(2,1)S(1)} %collective-permute-done.33), channel_id=1, source_target_pairs={{0,1},{1,2},{2,3},{3,4},{4,5},{5,6},{6,7},{7,0},{8,9},{9,10},{10,1... | collective-permute-start | bytes 393224 | tf_op jit(solution)/shard_map/while/body/eval_jaxpr/ppermute | solution.py:41
  390.8 6.2 %collective-permute-start.35 = (bf16[128,512]{1,0:T(8,128)(2,1)S(1)}, bf16[128,512]{1,0:T(8,128)(2,1)S(1)}, u32[]{:S(2)}, u32[]{:S(2)}) collective-permute-start(bf16[128,512]{1,0:T(8,128)(2,1)S(1)} %collective-permute-done.34), channel_id=1, source_target_pairs={{0,1},{1,2},{2,3},{3,4},{4,5},{5,6},{6,7},{7,0},{8,9},{9,10},{10,1... | collective-permute-start | bytes 393224 | tf_op jit(solution)/shard_map/while/body/eval_jaxpr/ppermute | solution.py:41
  397.7 6.3 %collective-permute-start.36 = (bf16[128,512]{1,0:T(8,128)(2,1)S(1)}, bf16[128,512]{1,0:T(8,128)(2,1)}, u32[]{:S(2)}, u32[]{:S(2)}) collective-permute-start(bf16[128,512]{1,0:T(8,128)(2,1)S(1)} %collective-permute-done.35), channel_id=1, source_target_pairs={{0,1},{1,2},{2,3},{3,4},{4,5},{5,6},{6,7},{7,0},{8,9},{9,10},{10,1... | collective-permute-start | bytes 393224 | tf_op jit(solution)/shard_map/while/body/eval_jaxpr/ppermute | solution.py:41
  404.0 6.5 %collective-permute-start.37 = (bf16[128,512]{1,0:T(8,128)(2,1)}, bf16[128,512]{1,0:T(8,128)(2,1)}, u32[]{:S(2)}, u32[]{:S(2)}) collective-permute-start(bf16[128,512]{1,0:T(8,128)(2,1)} %collective-permute-done.36), channel_id=1, source_target_pairs={{0,1},{1,2},{2,3},{3,4},{4,5},{5,6},{6,7},{7,0},{8,9},{9,10},{10,1... | collective-permute-start | bytes 393224 | tf_op jit(solution)/shard_map/while/body/eval_jaxpr/ppermute | solution.py:41
  410.5 6.5 %collective-permute-start.38 = (bf16[128,512]{1,0:T(8,128)(2,1)}, bf16[128,512]{1,0:T(8,128)(2,1)}, u32[]{:S(2)}, u32[]{:S(2)}) collective-permute-start(bf16[128,512]{1,0:T(8,128)(2,1)} %collective-permute-done.37), channel_id=1, source_target_pairs={{0,1},{1,2},{2,3},{3,4},{4,5},{5,6},{6,7},{7,0},{8,9},{9,10},{10,1... | collective-permute-start | bytes 393224 | tf_op jit(solution)/shard_map/while/body/eval_jaxpr/ppermute | solution.py:41
  412.5 6.5 %collective-permute-start.32 = (bf16[1,128,512]{2,1,0:T(8,128)(2,1)}, bf16[1,128,512]{2,1,0:T(8,128)(2,1)S(1)}, u32[]{:S(2)}, u32[]{:S(2)}) collective-permute-start(bf16[1,128,512]{2,1,0:T(8,128)(2,1)} %get-tuple-element.100), channel_id=1, source_target_pairs={{0,8},{8,16},{16,24},{1,9},{9,17},{17,25},{2,10},{10,18},{18,26},{... | collective-permute-start | bytes 393224 | tf_op jit(solution)/shard_map/ppermute | solution.py:10
  417.0 6.4 %collective-permute-start.39 = (bf16[128,512]{1,0:T(8,128)(2,1)}, bf16[128,512]{1,0:T(8,128)(2,1)S(1)}, u32[]{:S(2)}, u32[]{:S(2)}) collective-permute-start(bf16[128,512]{1,0:T(8,128)(2,1)} %collective-permute-done.38), channel_id=1, source_target_pairs={{0,1},{1,2},{2,3},{3,4},{4,5},{5,6},{6,7},{7,0},{8,9},{9,10},{10,1... | collective-permute-start | bytes 393224 | tf_op jit(solution)/shard_map/while/body/eval_jaxpr/ppermute | solution.py:41
  419.7 103.7 %all-gather.19.cloned.1.call-start = ((), (), s32[]{:S(2)}) async-start(), calls=%async_computation.5 | async-start | bytes 1179648 | tf_op jit(solution)/shard_map/all_gather | solution.py:72
  460.8 6.2 %collective-permute-start.41 = (bf16[128,512]{1,0:T(8,128)(2,1)S(1)}, bf16[128,512]{1,0:T(8,128)(2,1)S(1)}, u32[]{:S(2)}, u32[]{:S(2)}) collective-permute-start(bf16[128,512]{1,0:T(8,128)(2,1)S(1)} %fusion.129), channel_id=1, source_target_pairs={{0,1},{1,2},{2,3},{3,4},{4,5},{5,6},{6,7},{7,0},{8,9},{9,10},{10,1... | collective-permute-start | bytes 393224 | tf_op jit(solution)/shard_map/while/body/eval_jaxpr/ppermute | solution.py:41
  485.6 6.3 %collective-permute-start.45 = (bf16[128,512]{1,0:T(8,128)(2,1)S(1)}, bf16[128,512]{1,0:T(8,128)(2,1)}, u32[]{:S(2)}, u32[]{:S(2)}) collective-permute-start(bf16[128,512]{1,0:T(8,128)(2,1)S(1)} %collective-permute-done.44), channel_id=1, source_target_pairs={{0,1},{1,2},{2,3},{3,4},{4,5},{5,6},{6,7},{7,0},{8,9},{9,10},{10,1... | collective-permute-start | bytes 393224 | tf_op jit(solution)/shard_map/while/body/eval_jaxpr/ppermute | solution.py:41
  491.9 6.5 %collective-permute-start.46 = (bf16[128,512]{1,0:T(8,128)(2,1)}, bf16[128,512]{1,0:T(8,128)(2,1)}, u32[]{:S(2)}, u32[]{:S(2)}) collective-permute-start(bf16[128,512]{1,0:T(8,128)(2,1)} %collective-permute-done.45), channel_id=1, source_target_pairs={{0,1},{1,2},{2,3},{3,4},{4,5},{5,6},{6,7},{7,0},{8,9},{9,10},{10,1... | collective-permute-start | bytes 393224 | tf_op jit(solution)/shard_map/while/body/eval_jaxpr/ppermute | solution.py:41
  493.3 6.2 %collective-permute-start.40 = (bf16[1,128,512]{2,1,0:T(8,128)(2,1)S(1)}, bf16[1,128,512]{2,1,0:T(8,128)(2,1)}, u32[]{:S(2)}, u32[]{:S(2)}) collective-permute-start(bf16[1,128,512]{2,1,0:T(8,128)(2,1)S(1)} %get-tuple-element.96), channel_id=1, source_target_pairs={{0,8},{8,16},{16,24},{1,9},{9,17},{17,25},{2,10},{10,18},{18,26},{... | collective-permute-start | bytes 393224 | tf_op jit(solution)/shard_map/ppermute | solution.py:10
  498.4 6.8 %collective-permute-start.47 = (bf16[128,512]{1,0:T(8,128)(2,1)}, bf16[128,512]{1,0:T(8,128)(2,1)}, u32[]{:S(2)}, u32[]{:S(2)}) collective-permute-start(bf16[128,512]{1,0:T(8,128)(2,1)} %collective-permute-done.46), channel_id=1, source_target_pairs={{0,1},{1,2},{2,3},{3,4},{4,5},{5,6},{6,7},{7,0},{8,9},{9,10},{10,1... | collective-permute-start | bytes 393224 | tf_op jit(solution)/shard_map/while/body/eval_jaxpr/ppermute | solution.py:41
  (39 other events, 863.9 us)
Sparse Core Ops, SparseCore 0:
  9.6 24.9 all-gather.20
  93.8 23.4 all-gather.8
  173.9 23.7 all-gather.10
  255.2 23.2 all-gather.12
  335.6 23.2 all-gather.14
  419.8 23.0 all-gather.16
  499.7 23.6 all-gather.18
